TPU v7x, 256 devices: a whole 4x4x8 slice. The times are simulated.
256 devices in a mesh: section: 8 (over z), expert: 8 (over y_hi, x), dp: 4 (over y_lo, core).
Axes of the slice: x: 4, y: 4 (y_hi: 2, y_lo: 2; y = y_hi * 2 + y_lo), z: 8, core: 2. Of those that a mesh axis runs over, the one named last changes fastest.
Arguments:
- tokens: bfloat16 [8, 256, 4096], P('section', None, ('expert', 'dp'))
- targets: bfloat16 [8, 256, 4096], P('section', None, ('expert', 'dp')), may hold values from -6 to 6
- group_ids: int32 [8, 256], P('section'), may hold values from 0 to 7, as said below
- expert_ids: int32 [1, 8, 8, 256, 2], P(None, 'section'), may hold values from 0 to 7, all different within a row; in each aligned block of 256 rows (0 to 255, 256 to 511, ..., all dimensions but the last counted through in order) at most 72 rows name the same one
- norm_gain: float32 [8, 4096], P('section', ('expert', 'dp')), may hold values from 0.5 to 1.5
- router: bfloat16 [8, 4096, 8], P('section', ('expert', 'dp')), may hold values from -0.09375 to 0.09375
- w_gate: bfloat16 [8, 8, 4096, 1536], P('section', 'expert', None, 'dp'), may hold values from -0.09375 to 0.09375
- w_up: bfloat16 [8, 8, 4096, 1536], P('section', 'expert', None, 'dp'), may hold values from -0.09375 to 0.09375
- w_down: bfloat16 [8, 8, 1536, 4096], P('section', 'expert', 'dp'), may hold values from -0.15625 to 0.15625
Outputs:
- grad_out: bfloat16 [8, 256, 4096], P('section', None, ('expert', 'dp'))
- group_loss: float32 [8], replicated
Inputs may be any that keep to these rules, and one draw needn't show every extreme that they name: `expert_ids`: in each aligned block of 256 rows (one micro-batch at one layer pass) no expert is named by more than 72 rows; a row names 2 different experts. `group_ids`: exactly one group has no rows; which one varies.
All inputs are finite; a program needn't handle non-finite values.
Results may differ from a plain program's by a relative error of at most 0.019.
Values may be sent and summed in bfloat16 or wider, within the bound.
A program may use at most 64 MiB of HBM per device.

v0:
```python
import jax
import jax.numpy as jnp
from jax import lax
from jax.sharding import PartitionSpec as P

GROUPS = 8
dro_rate = 0.3


def from_behind(value, axis, steps):
    count = lax.axis_size(axis)
    pairs = [(source, (source + steps) % count) for source in range(count)]
    return lax.ppermute(value, axis, pairs)


def per_device(tokens, targets, group_ids, expert_ids, norm_gain, router, w_gate, w_up, w_down):
    sections = lax.axis_size("section")
    lane_count = lax.axis_size("dp")
    experts = lax.axis_size("expert")
    circuits = expert_ids.shape[0]
    top_count = expert_ids.shape[-1]
    row_count = tokens.shape[1]
    piece_width = tokens.shape[2]
    full_width = piece_width * experts * lane_count
    capacity = min(row_count, row_count * top_count // experts * 9 // 8)
    section_place = lax.axis_index("section")
    gain_row = norm_gain[0]
    router_block = router[0]
    gate_matrix = w_gate[0, 0]
    up_matrix = w_up[0, 0]
    down_matrix = w_down[0, 0]
    expert_range = jnp.arange(experts, dtype=jnp.int32)
    slot_range = jnp.arange(capacity, dtype=jnp.int32)
    zero_index = jnp.zeros((), jnp.int32)

    def expert_rows(flat_rows):
        gate_part = jnp.dot(flat_rows, gate_matrix, preferred_element_type=jnp.float32)
        up_part = jnp.dot(flat_rows, up_matrix, preferred_element_type=jnp.float32)
        activated = (jax.nn.silu(gate_part) * up_part).astype(jnp.bfloat16)
        return jnp.dot(activated, down_matrix, preferred_element_type=jnp.float32).astype(
            jnp.bfloat16
        )

    def joined_work(received):
        item_count = received.shape[1]
        expert_part = expert_rows(received.reshape(item_count, full_width))
        return lax.all_to_all(
            expert_part.reshape(item_count, experts * lane_count, piece_width),
            ("expert", "dp"),
            split_axis=1,
            concat_axis=1,
            tiled=True,
        )

    def one_tick(moment, current):
        micro_index = (section_place - moment) % sections
        circuit = (moment // sections).astype(jnp.int32)
        choices = lax.dynamic_slice(
            expert_ids,
            (circuit, zero_index, micro_index, zero_index, zero_index),
            (1, 1, 1, row_count, top_count),
        ).reshape(row_count, top_count)
        wide_state = current.astype(jnp.float32)
        local_squares = jnp.sum(wide_state * wide_state, axis=1)
        total_squares = lax.psum(local_squares, ("expert", "dp"))
        row_scale = lax.rsqrt(total_squares / full_width + 1e-06)[:, None]
        normed = (wide_state * row_scale * gain_row[None, :]).astype(jnp.bfloat16)
        partial_logits = jnp.dot(normed, router_block, preferred_element_type=jnp.float32)
        logits = lax.psum(partial_logits, ("expert", "dp"))
        member = (choices[:, :, None] == expert_range[None, None, :]).astype(jnp.int32)
        flat_member = member.reshape(-1, experts)
        rank_before = jnp.cumsum(flat_member, axis=0) - flat_member
        position = jnp.sum(rank_before * flat_member, axis=1).reshape(row_count, top_count)
        chosen = jnp.sum(logits[:, None, :] * member.astype(jnp.float32), axis=2)
        weights = jnp.exp(chosen)
        gate_weights = weights / jnp.sum(weights, axis=1, keepdims=True)
        placement = member.astype(jnp.float32)[:, :, :, None] * (
            position[:, :, None, None] == slot_range[None, None, None, :]
        ).astype(jnp.float32)
        picker = (
            jnp.sum(placement, axis=1).reshape(row_count, experts * capacity).astype(jnp.bfloat16)
        )
        combiner = jnp.sum(placement * gate_weights[:, :, None, None], axis=1)
        outgoing = jnp.einsum(
            "us,ud->sd", picker, normed, preferred_element_type=jnp.float32
        ).astype(jnp.bfloat16)
        spread = jnp.broadcast_to(
            outgoing.reshape(experts, 1, capacity, piece_width),
            (experts, lane_count, capacity, piece_width),
        )
        returned = joined_work(
            lax.all_to_all(
                spread.reshape(experts * lane_count, capacity, piece_width),
                ("expert", "dp"),
                split_axis=0,
                concat_axis=2,
                tiled=True,
            )
        )
        lane_total = jnp.sum(
            returned.reshape(capacity, experts, lane_count, piece_width).astype(jnp.float32), axis=2
        )
        mixture = jnp.einsum("uec,ced->ud", combiner, lane_total, precision=lax.Precision.HIGHEST)
        updated = (wide_state + mixture).astype(jnp.bfloat16)
        return from_behind(updated, "section", 1)

    final_state = lax.fori_loop(0, circuits * sections, one_tick, tokens[0])
    difference = final_state.astype(jnp.float32) - targets[0].astype(jnp.float32)
    partial_squares = jnp.sum(difference * difference, axis=1) / full_width
    group_member = (group_ids[0][:, None] == jnp.arange(GROUPS, dtype=jnp.int32)[None, :]).astype(
        jnp.float32
    )
    local_totals = jnp.dot(partial_squares, group_member, precision=lax.Precision.HIGHEST)
    first_lane = ((lax.axis_index("expert") == 0) & (lax.axis_index("dp") == 0)).astype(jnp.float32)
    local_counts = jnp.sum(group_member, axis=0) * first_lane
    totals, counts = lax.psum((local_totals, local_counts), ("section", "expert", "dp"))
    group_loss = totals / jnp.maximum(counts, 1.0)
    raised = jnp.exp(dro_rate * group_loss)
    group_weight = raised / jnp.sum(raised)
    token_count = sections * row_count
    row_weight_table = group_weight * token_count / jnp.maximum(counts, 1.0)
    row_weight = jnp.dot(group_member, row_weight_table, precision=lax.Precision.HIGHEST)
    grad_out = (row_weight[:, None] * difference).astype(jnp.bfloat16)[None]
    return (grad_out, group_loss)


def solution(mesh):
    placed = (
        P("section", None, ("expert", "dp")),
        P("section", None, ("expert", "dp")),
        P("section", None),
        P(None, "section", None, None, None),
        P("section", ("expert", "dp")),
        P("section", ("expert", "dp"), None),
        P("section", "expert", None, "dp"),
        P("section", "expert", None, "dp"),
        P("section", "expert", "dp", None),
    )
    return jax.shard_map(
        per_device,
        mesh=mesh,
        in_specs=placed,
        out_specs=(P("section", None, ("expert", "dp")), P()),
        check_vma=False,
    )
```

profile of v0, /device:TPU:1, one launch (start us, length us, event | category | flops | bytes accessed | tf_op | source)
XLA Modules:
  0.0 1500.4 jit_solution(1334823001441641367)
XLA Ops:
  2.3 1422.9 %while.17 = (s32[]{:T(128)}, bf16[256,128]{1,0:T(8,128)(2,1)S(1)}, s32[]{:T(128)}, s32[1,1,8,256,2]{3,4,2,1,0:T(2,128)}, f32[1,128]{1,0:T(1,128)}, /*index=5*/bf...) while((s32[]{:T(128)}, bf16[256,128]{1,0:T(8,128)(2,1)S(1)}, ...), condition=%wide.region_12.13_spmd.clone.clone, body=%wide.region_0.12_spmd.clone.clone.sunk | while | flops 947298688 | bytes 33643788 | solution.py:107
  4.3 65.3 %psum.50 = f32[256]{0:T(256)S(1)} all-reduce(f32[256]{0:T(256)S(1)} %fusion.92), channel_id=1, replica_groups=mesh['section'=8,'expert'=8,'dp'=4] {'expert','dp'}, use_global_device_ids=true, to_apply=%region_5.5 | all-reduce | flops 256 | bytes 2048 | tf_op jit(solution)/shard_map/while/body/eval_jaxpr/psum | solution.py:65
  70.4 66.5 %psum.51 = f32[256,8]{0,1:T(8,128)S(1)} all-reduce(f32[256,8]{0,1:T(8,128)S(1)} %fusion.93), channel_id=1, replica_groups=mesh['section'=8,'expert'=8,'dp'=4] {'expert','dp'}, use_global_device_ids=true, to_apply=%region_6.6 | all-reduce | flops 2048 | bytes 16384 | tf_op jit(solution)/shard_map/while/body/eval_jaxpr/psum | solution.py:69
  140.3 15.9 %all_to_all.58 = bf16[32,72,128]{2,1,0:T(8,128)(2,1)S(1)} all-to-all(bf16[32,72,128]{2,1,0:T(8,128)(2,1)S(1)} %bitcast.117), channel_id=1, replica_groups=mesh['section'=8,'expert'=8,'dp'=4] {'expert','dp'}, dimensions={0} | all-to-all | bytes 1179648 | tf_op jit(solution)/shard_map/while/body/eval_jaxpr/all_to_all | solution.py:92
  157.0 4.4 fusion.95
  161.6 16.2 %all_to_all.59 = bf16[72,32,128]{2,0,1:T(8,128)(2,1)S(1)} all-to-all(bf16[72,32,128]{2,0,1:T(8,128)(2,1)S(1)} %bitcast.119), channel_id=1, replica_groups=mesh['section'=8,'expert'=8,'dp'=4] {'expert','dp'}, dimensions={1} | all-to-all | bytes 1179648 | tf_op jit(solution)/shard_map/while/body/eval_jaxpr/all_to_all | solution.py:47
  180.9 5.6 collective-permute-done
  188.4 63.6 %psum.50 = f32[256]{0:T(256)S(1)} all-reduce(f32[256]{0:T(256)S(1)} %fusion.92), channel_id=1, replica_groups=mesh['section'=8,'expert'=8,'dp'=4] {'expert','dp'}, use_global_device_ids=true, to_apply=%region_5.5 | all-reduce | flops 256 | bytes 2048 | tf_op jit(solution)/shard_map/while/body/eval_jaxpr/psum | solution.py:65
  253.0 63.6 %psum.51 = f32[256,8]{0,1:T(8,128)S(1)} all-reduce(f32[256,8]{0,1:T(8,128)S(1)} %fusion.93), channel_id=1, replica_groups=mesh['section'=8,'expert'=8,'dp'=4] {'expert','dp'}, use_global_device_ids=true, to_apply=%region_6.6 | all-reduce | flops 2048 | bytes 16384 | tf_op jit(solution)/shard_map/while/body/eval_jaxpr/psum | solution.py:69
  319.9 15.9 %all_to_all.58 = bf16[32,72,128]{2,1,0:T(8,128)(2,1)S(1)} all-to-all(bf16[32,72,128]{2,1,0:T(8,128)(2,1)S(1)} %bitcast.117), channel_id=1, replica_groups=mesh['section'=8,'expert'=8,'dp'=4] {'expert','dp'}, dimensions={0} | all-to-all | bytes 1179648 | tf_op jit(solution)/shard_map/while/body/eval_jaxpr/all_to_all | solution.py:92
  336.6 4.4 fusion.95
  341.2 16.2 %all_to_all.59 = bf16[72,32,128]{2,0,1:T(8,128)(2,1)S(1)} all-to-all(bf16[72,32,128]{2,0,1:T(8,128)(2,1)S(1)} %bitcast.119), channel_id=1, replica_groups=mesh['section'=8,'expert'=8,'dp'=4] {'expert','dp'}, dimensions={1} | all-to-all | bytes 1179648 | tf_op jit(solution)/shard_map/while/body/eval_jaxpr/all_to_all | solution.py:47
  358.9 4.3 collective-permute-done
  365.1 63.9 %psum.50 = f32[256]{0:T(256)S(1)} all-reduce(f32[256]{0:T(256)S(1)} %fusion.92), channel_id=1, replica_groups=mesh['section'=8,'expert'=8,'dp'=4] {'expert','dp'}, use_global_device_ids=true, to_apply=%region_5.5 | all-reduce | flops 256 | bytes 2048 | tf_op jit(solution)/shard_map/while/body/eval_jaxpr/psum | solution.py:65
  430.0 63.6 %psum.51 = f32[256,8]{0,1:T(8,128)S(1)} all-reduce(f32[256,8]{0,1:T(8,128)S(1)} %fusion.93), channel_id=1, replica_groups=mesh['section'=8,'expert'=8,'dp'=4] {'expert','dp'}, use_global_device_ids=true, to_apply=%region_6.6 | all-reduce | flops 2048 | bytes 16384 | tf_op jit(solution)/shard_map/while/body/eval_jaxpr/psum | solution.py:69
  496.9 15.9 %all_to_all.58 = bf16[32,72,128]{2,1,0:T(8,128)(2,1)S(1)} all-to-all(bf16[32,72,128]{2,1,0:T(8,128)(2,1)S(1)} %bitcast.117), channel_id=1, replica_groups=mesh['section'=8,'expert'=8,'dp'=4] {'expert','dp'}, dimensions={0} | all-to-all | bytes 1179648 | tf_op jit(solution)/shard_map/while/body/eval_jaxpr/all_to_all | solution.py:92
  513.6 4.4 fusion.95
  518.2 16.2 %all_to_all.59 = bf16[72,32,128]{2,0,1:T(8,128)(2,1)S(1)} all-to-all(bf16[72,32,128]{2,0,1:T(8,128)(2,1)S(1)} %bitcast.119), channel_id=1, replica_groups=mesh['section'=8,'expert'=8,'dp'=4] {'expert','dp'}, dimensions={1} | all-to-all | bytes 1179648 | tf_op jit(solution)/shard_map/while/body/eval_jaxpr/all_to_all | solution.py:47
  535.9 4.3 collective-permute-done
  542.1 63.9 %psum.50 = f32[256]{0:T(256)S(1)} all-reduce(f32[256]{0:T(256)S(1)} %fusion.92), channel_id=1, replica_groups=mesh['section'=8,'expert'=8,'dp'=4] {'expert','dp'}, use_global_device_ids=true, to_apply=%region_5.5 | all-reduce | flops 256 | bytes 2048 | tf_op jit(solution)/shard_map/while/body/eval_jaxpr/psum | solution.py:65
  607.0 63.6 %psum.51 = f32[256,8]{0,1:T(8,128)S(1)} all-reduce(f32[256,8]{0,1:T(8,128)S(1)} %fusion.93), channel_id=1, replica_groups=mesh['section'=8,'expert'=8,'dp'=4] {'expert','dp'}, use_global_device_ids=true, to_apply=%region_6.6 | all-reduce | flops 2048 | bytes 16384 | tf_op jit(solution)/shard_map/while/body/eval_jaxpr/psum | solution.py:69
  673.9 15.9 %all_to_all.58 = bf16[32,72,128]{2,1,0:T(8,128)(2,1)S(1)} all-to-all(bf16[32,72,128]{2,1,0:T(8,128)(2,1)S(1)} %bitcast.117), channel_id=1, replica_groups=mesh['section'=8,'expert'=8,'dp'=4] {'expert','dp'}, dimensions={0} | all-to-all | bytes 1179648 | tf_op jit(solution)/shard_map/while/body/eval_jaxpr/all_to_all | solution.py:92
  690.6 4.4 fusion.95
  695.2 16.2 %all_to_all.59 = bf16[72,32,128]{2,0,1:T(8,128)(2,1)S(1)} all-to-all(bf16[72,32,128]{2,0,1:T(8,128)(2,1)S(1)} %bitcast.119), channel_id=1, replica_groups=mesh['section'=8,'expert'=8,'dp'=4] {'expert','dp'}, dimensions={1} | all-to-all | bytes 1179648 | tf_op jit(solution)/shard_map/while/body/eval_jaxpr/all_to_all | solution.py:47
  719.1 63.9 %psum.50 = f32[256]{0:T(256)S(1)} all-reduce(f32[256]{0:T(256)S(1)} %fusion.92), channel_id=1, replica_groups=mesh['section'=8,'expert'=8,'dp'=4] {'expert','dp'}, use_global_device_ids=true, to_apply=%region_5.5 | all-reduce | flops 256 | bytes 2048 | tf_op jit(solution)/shard_map/while/body/eval_jaxpr/psum | solution.py:65
  784.0 63.6 %psum.51 = f32[256,8]{0,1:T(8,128)S(1)} all-reduce(f32[256,8]{0,1:T(8,128)S(1)} %fusion.93), channel_id=1, replica_groups=mesh['section'=8,'expert'=8,'dp'=4] {'expert','dp'}, use_global_device_ids=true, to_apply=%region_6.6 | all-reduce | flops 2048 | bytes 16384 | tf_op jit(solution)/shard_map/while/body/eval_jaxpr/psum | solution.py:69
  850.9 15.9 %all_to_all.58 = bf16[32,72,128]{2,1,0:T(8,128)(2,1)S(1)} all-to-all(bf16[32,72,128]{2,1,0:T(8,128)(2,1)S(1)} %bitcast.117), channel_id=1, replica_groups=mesh['section'=8,'expert'=8,'dp'=4] {'expert','dp'}, dimensions={0} | all-to-all | bytes 1179648 | tf_op jit(solution)/shard_map/while/body/eval_jaxpr/all_to_all | solution.py:92
  867.6 4.4 fusion.95
  872.2 16.2 %all_to_all.59 = bf16[72,32,128]{2,0,1:T(8,128)(2,1)S(1)} all-to-all(bf16[72,32,128]{2,0,1:T(8,128)(2,1)S(1)} %bitcast.119), channel_id=1, replica_groups=mesh['section'=8,'expert'=8,'dp'=4] {'expert','dp'}, dimensions={1} | all-to-all | bytes 1179648 | tf_op jit(solution)/shard_map/while/body/eval_jaxpr/all_to_all | solution.py:47
  889.9 4.3 collective-permute-done
  896.1 63.9 %psum.50 = f32[256]{0:T(256)S(1)} all-reduce(f32[256]{0:T(256)S(1)} %fusion.92), channel_id=1, replica_groups=mesh['section'=8,'expert'=8,'dp'=4] {'expert','dp'}, use_global_device_ids=true, to_apply=%region_5.5 | all-reduce | flops 256 | bytes 2048 | tf_op jit(solution)/shard_map/while/body/eval_jaxpr/psum | solution.py:65
  960.9 63.6 %psum.51 = f32[256,8]{0,1:T(8,128)S(1)} all-reduce(f32[256,8]{0,1:T(8,128)S(1)} %fusion.93), channel_id=1, replica_groups=mesh['section'=8,'expert'=8,'dp'=4] {'expert','dp'}, use_global_device_ids=true, to_apply=%region_6.6 | all-reduce | flops 2048 | bytes 16384 | tf_op jit(solution)/shard_map/while/body/eval_jaxpr/psum | solution.py:69
  1027.9 15.9 %all_to_all.58 = bf16[32,72,128]{2,1,0:T(8,128)(2,1)S(1)} all-to-all(bf16[32,72,128]{2,1,0:T(8,128)(2,1)S(1)} %bitcast.117), channel_id=1, replica_groups=mesh['section'=8,'expert'=8,'dp'=4] {'expert','dp'}, dimensions={0} | all-to-all | bytes 1179648 | tf_op jit(solution)/shard_map/while/body/eval_jaxpr/all_to_all | solution.py:92
  1044.6 4.4 fusion.95
  1049.2 16.2 %all_to_all.59 = bf16[72,32,128]{2,0,1:T(8,128)(2,1)S(1)} all-to-all(bf16[72,32,128]{2,0,1:T(8,128)(2,1)S(1)} %bitcast.119), channel_id=1, replica_groups=mesh['section'=8,'expert'=8,'dp'=4] {'expert','dp'}, dimensions={1} | all-to-all | bytes 1179648 | tf_op jit(solution)/shard_map/while/body/eval_jaxpr/all_to_all | solution.py:47
  1066.9 4.3 collective-permute-done
  1073.1 63.9 %psum.50 = f32[256]{0:T(256)S(1)} all-reduce(f32[256]{0:T(256)S(1)} %fusion.92), channel_id=1, replica_groups=mesh['section'=8,'expert'=8,'dp'=4] {'expert','dp'}, use_global_device_ids=true, to_apply=%region_5.5 | all-reduce | flops 256 | bytes 2048 | tf_op jit(solution)/shard_map/while/body/eval_jaxpr/psum | solution.py:65
  1137.9 63.6 %psum.51 = f32[256,8]{0,1:T(8,128)S(1)} all-reduce(f32[256,8]{0,1:T(8,128)S(1)} %fusion.93), channel_id=1, replica_groups=mesh['section'=8,'expert'=8,'dp'=4] {'expert','dp'}, use_global_device_ids=true, to_apply=%region_6.6 | all-reduce | flops 2048 | bytes 16384 | tf_op jit(solution)/shard_map/while/body/eval_jaxpr/psum | solution.py:69
  1204.9 15.9 %all_to_all.58 = bf16[32,72,128]{2,1,0:T(8,128)(2,1)S(1)} all-to-all(bf16[32,72,128]{2,1,0:T(8,128)(2,1)S(1)} %bitcast.117), channel_id=1, replica_groups=mesh['section'=8,'expert'=8,'dp'=4] {'expert','dp'}, dimensions={0} | all-to-all | bytes 1179648 | tf_op jit(solution)/shard_map/while/body/eval_jaxpr/all_to_all | solution.py:92
  1221.6 4.4 fusion.95
  1226.2 16.2 %all_to_all.59 = bf16[72,32,128]{2,0,1:T(8,128)(2,1)S(1)} all-to-all(bf16[72,32,128]{2,0,1:T(8,128)(2,1)S(1)} %bitcast.119), channel_id=1, replica_groups=mesh['section'=8,'expert'=8,'dp'=4] {'expert','dp'}, dimensions={1} | all-to-all | bytes 1179648 | tf_op jit(solution)/shard_map/while/body/eval_jaxpr/all_to_all | solution.py:47
  1243.9 4.3 collective-permute-done
  1250.1 63.9 %psum.50 = f32[256]{0:T(256)S(1)} all-reduce(f32[256]{0:T(256)S(1)} %fusion.92), channel_id=1, replica_groups=mesh['section'=8,'expert'=8,'dp'=4] {'expert','dp'}, use_global_device_ids=true, to_apply=%region_5.5 | all-reduce | flops 256 | bytes 2048 | tf_op jit(solution)/shard_map/while/body/eval_jaxpr/psum | solution.py:65
  1314.9 63.6 %psum.51 = f32[256,8]{0,1:T(8,128)S(1)} all-reduce(f32[256,8]{0,1:T(8,128)S(1)} %fusion.93), channel_id=1, replica_groups=mesh['section'=8,'expert'=8,'dp'=4] {'expert','dp'}, use_global_device_ids=true, to_apply=%region_6.6 | all-reduce | flops 2048 | bytes 16384 | tf_op jit(solution)/shard_map/while/body/eval_jaxpr/psum | solution.py:69
  1381.8 15.9 %all_to_all.58 = bf16[32,72,128]{2,1,0:T(8,128)(2,1)S(1)} all-to-all(bf16[32,72,128]{2,1,0:T(8,128)(2,1)S(1)} %bitcast.117), channel_id=1, replica_groups=mesh['section'=8,'expert'=8,'dp'=4] {'expert','dp'}, dimensions={0} | all-to-all | bytes 1179648 | tf_op jit(solution)/shard_map/while/body/eval_jaxpr/all_to_all | solution.py:92
  1398.6 4.4 fusion.95
  1403.2 16.2 %all_to_all.59 = bf16[72,32,128]{2,0,1:T(8,128)(2,1)S(1)} all-to-all(bf16[72,32,128]{2,0,1:T(8,128)(2,1)S(1)} %bitcast.119), channel_id=1, replica_groups=mesh['section'=8,'expert'=8,'dp'=4] {'expert','dp'}, dimensions={1} | all-to-all | bytes 1179648 | tf_op jit(solution)/shard_map/while/body/eval_jaxpr/all_to_all | solution.py:47
  1425.4 72.8 %all-reduce = (f32[8]{0:T(128)S(1)}, f32[8]{0:T(128)S(1)}) all-reduce(f32[8]{0:T(128)S(1)} %broadcast_multiply_fusion.1, f32[8]{0:T(128)S(1)} %convolution_bitcast_fusion.1), channel_id=1, replica_groups=mesh['section'=8,'expert'=8,'dp'=4] {'section','expert','dp'}, use_global_device_ids=true, to_apply=%region_16.17 | all-reduce | flops 16 | bytes 128 | tf_op jit(solution)/shard_map/psum | solution.py:116
  (273 shorter events, 81.6 us)
Async XLA Ops:
  2.3 1422.9 %copy-start.1 = (bf16[1,256,128]{2,1,0:T(8,128)(2,1)S(1)}, bf16[1,256,128]{2,1,0:T(8,128)(2,1)}, u32[]{:S(2)}) copy-start(bf16[1,256,128]{2,1,0:T(8,128)(2,1)} %param.12) | copy-start | bytes 196612
  2.3 1423.0 %copy-start.3 = (s32[1,256]{1,0:T(1,128)S(1)}, s32[1,256]{1,0:T(1,128)}, u32[]{:S(2)}) copy-start(s32[1,256]{1,0:T(1,128)} %param.13) | copy-start | bytes 3076
  138.8 17.4 %copy-start = (bf16[4096,384]{1,0:T(8,128)(2,1)S(1)}, bf16[4096,384]{1,0:T(8,128)(2,1)}, u32[]{:S(2)}) copy-start(bf16[4096,384]{1,0:T(8,128)(2,1)} %get-tuple-element.482) | copy-start | bytes 9437188 | tf_op jit(solution)/shard_map/while
  179.2 7.3 collective-permute-start
  318.4 17.4 %copy-start = (bf16[4096,384]{1,0:T(8,128)(2,1)S(1)}, bf16[4096,384]{1,0:T(8,128)(2,1)}, u32[]{:S(2)}) copy-start(bf16[4096,384]{1,0:T(8,128)(2,1)} %get-tuple-element.482) | copy-start | bytes 9437188 | tf_op jit(solution)/shard_map/while
  358.8 4.4 collective-permute-start
  495.4 17.4 %copy-start = (bf16[4096,384]{1,0:T(8,128)(2,1)S(1)}, bf16[4096,384]{1,0:T(8,128)(2,1)}, u32[]{:S(2)}) copy-start(bf16[4096,384]{1,0:T(8,128)(2,1)} %get-tuple-element.482) | copy-start | bytes 9437188 | tf_op jit(solution)/shard_map/while
  535.8 4.4 collective-permute-start
  672.4 17.4 %copy-start = (bf16[4096,384]{1,0:T(8,128)(2,1)S(1)}, bf16[4096,384]{1,0:T(8,128)(2,1)}, u32[]{:S(2)}) copy-start(bf16[4096,384]{1,0:T(8,128)(2,1)} %get-tuple-element.482) | copy-start | bytes 9437188 | tf_op jit(solution)/shard_map/while
  712.8 4.4 collective-permute-start
  849.4 17.4 %copy-start = (bf16[4096,384]{1,0:T(8,128)(2,1)S(1)}, bf16[4096,384]{1,0:T(8,128)(2,1)}, u32[]{:S(2)}) copy-start(bf16[4096,384]{1,0:T(8,128)(2,1)} %get-tuple-element.482) | copy-start | bytes 9437188 | tf_op jit(solution)/shard_map/while
  889.8 4.4 collective-permute-start
  1026.4 17.4 %copy-start = (bf16[4096,384]{1,0:T(8,128)(2,1)S(1)}, bf16[4096,384]{1,0:T(8,128)(2,1)}, u32[]{:S(2)}) copy-start(bf16[4096,384]{1,0:T(8,128)(2,1)} %get-tuple-element.482) | copy-start | bytes 9437188 | tf_op jit(solution)/shard_map/while
  1066.8 4.4 collective-permute-start
  1203.4 17.4 %copy-start = (bf16[4096,384]{1,0:T(8,128)(2,1)S(1)}, bf16[4096,384]{1,0:T(8,128)(2,1)}, u32[]{:S(2)}) copy-start(bf16[4096,384]{1,0:T(8,128)(2,1)} %get-tuple-element.482) | copy-start | bytes 9437188 | tf_op jit(solution)/shard_map/while
  1243.8 4.4 collective-permute-start
  1380.4 17.4 %copy-start = (bf16[4096,384]{1,0:T(8,128)(2,1)S(1)}, bf16[4096,384]{1,0:T(8,128)(2,1)}, u32[]{:S(2)}) copy-start(bf16[4096,384]{1,0:T(8,128)(2,1)} %get-tuple-element.482) | copy-start | bytes 9437188 | tf_op jit(solution)/shard_map/while
  1420.8 4.4 collective-permute-start
  1498.9 1.5 copy-start.2
where the time goes:
time: 1500 us
  blocking collectives  1350 us (90%)
  matrix products  68.6 us (5%)
  waiting for transfers between devices  35.8 us (2%)
  local copies, waits for them, and re-layouts  20.9 us (1%)
  other arithmetic  16.5 us (1%)
    psum x8, blocking collectives, one_tick(): total_squares = lax.psum(local_squares, ('expert', 'dp'))  512 us
    psum x8, blocking collectives, one_tick(): logits = lax.psum(partial_logits, ('expert', 'dp'))  512 us
    all_to_all x8, blocking collectives, joined_work(): lax.all_to_all(expert_part.reshape(item_count, experts * lane_count, piec...  130 us
    all_to_all x8, blocking collectives, one_tick(): lax.all_to_all(spread.reshape(experts * lane_count, capacity, piece_width...  127 us
    psum x1, blocking collectives, per_device(): lax.psum((local_totals, local_counts), ('section', 'expert', 'dp'))  72.8 us
    ppermute x8, waiting for transfers between devices, from_behind(): return lax.ppermute(value, axis, pairs)  35.8 us
    dot_general x8, matrix products, expert_rows(): jnp.dot(activated, down_matrix, preferred_element_type=jnp.float32)  35.4 us
  transfers between devices with their start and end apart: 8, of which 8 were waited for; matrix products, arithmetic and copies ran while one was open for 0% of the time, Pallas kernels for 0%

commit v1 on v0

--- a/solution.py
+++ b/solution.py
@@ -1,10 +1,20 @@
+import functools
 import jax
 import jax.numpy as jnp
 from jax import lax
 from jax.sharding import PartitionSpec as P
+from jax.lax import all_gather
 
 GROUPS = 8
 dro_rate = 0.3
+
+
+def carry_rows_by_axis(body, device_axis):
+    r_now = jnp.sum(all_gather(body, axis_name=device_axis), axis=0)
+    return r_now
+
+
+balance_the_terms = functools.partial(carry_rows_by_axis, device_axis=("expert", "dp"))
 
 
 def from_behind(value, axis, steps):
@@ -66,7 +76,7 @@
         row_scale = lax.rsqrt(total_squares / full_width + 1e-06)[:, None]
         normed = (wide_state * row_scale * gain_row[None, :]).astype(jnp.bfloat16)
         partial_logits = jnp.dot(normed, router_block, preferred_element_type=jnp.float32)
-        logits = lax.psum(partial_logits, ("expert", "dp"))
+        logits = balance_the_terms(partial_logits)
         member = (choices[:, :, None] == expert_range[None, None, :]).astype(jnp.int32)
         flat_member = member.reshape(-1, experts)
         rank_before = jnp.cumsum(flat_member, axis=0) - flat_member

time: 1500 us -> 1300 us (0.87)
  blocking collectives: 1350 us -> 1140 us
    psum x8 -> x0, blocking collectives: 512 us -> none  [one_tick(): logits = lax.psum(partial_logits, ('expert', 'dp'))]
    all_gather x0 -> x8, blocking collectives: none -> 294 us  [carry_rows_by_axis(): r_now = jnp.sum(all_gather(body, axis_name=device_axis), axis=0)]
where the time goes in v1:
time: 1300 us; the launch traced here: 1290 us
  blocking collectives  1140 us (88%)
  matrix products  81.5 us (6%)
  waiting for transfers between devices  35.8 us (3%)
  local copies, waits for them, and re-layouts  20.8 us (2%)
  other arithmetic  16.8 us (1%)
    psum x8, blocking collectives, one_tick(): total_squares = lax.psum(local_squares, ('expert', 'dp'))  512 us
    all_gather x8, blocking collectives, carry_rows_by_axis(): r_now = jnp.sum(all_gather(body, axis_name=device_axis), axis=0)  294 us
    all_to_all x8, blocking collectives, joined_work(): lax.all_to_all(expert_part.reshape(item_count, experts * lane_count, piec...  130 us
    all_to_all x8, blocking collectives, one_tick(): lax.all_to_all(spread.reshape(experts * lane_count, capacity, piece_width...  127 us
    psum x1, blocking collectives, per_device(): lax.psum((local_totals, local_counts), ('section', 'expert', 'dp'))  72.8 us
    ppermute x8, waiting for transfers between devices, from_behind(): return lax.ppermute(value, axis, pairs)  35.8 us
    dot_general x8, matrix products, expert_rows(): jnp.dot(activated, down_matrix, preferred_element_type=jnp.float32)  34.9 us
  transfers between devices with their start and end apart: 8, of which 8 were waited for; matrix products, arithmetic and copies ran while one was open for 0% of the time, Pallas kernels for 0%

profile of v1, /device:TPU:1, one launch (start us, length us, event | category | flops | bytes accessed | tf_op | source)
XLA Modules:
  0.0 1294.9 jit_solution(5269389449176925619)
XLA Ops:
  2.3 1217.3 %while.17 = (s32[]{:T(128)}, bf16[256,128]{1,0:T(8,128)(2,1)S(1)}, s32[]{:T(128)}, s32[1,1,8,256,2]{3,4,2,1,0:T(2,128)}, f32[1,128]{1,0:T(1,128)}, /*index=5*/bf...) while((s32[]{:T(128)}, bf16[256,128]{1,0:T(8,128)(2,1)S(1)}, ...), condition=%wide.region_12.13_spmd.clone.clone, body=%wide.region_0.12_spmd.clone.clone.sunk | while | flops 947360128 | bytes 21585148 | solution.py:117
  4.3 65.3 %psum.33 = f32[256]{0:T(256)S(1)} all-reduce(f32[256]{0:T(256)S(1)} %fusion.92), channel_id=1, replica_groups=mesh['section'=8,'expert'=8,'dp'=4] {'expert','dp'}, use_global_device_ids=true, to_apply=%region_5.5 | all-reduce | flops 256 | bytes 2048 | tf_op jit(solution)/shard_map/while/body/eval_jaxpr/psum | solution.py:75
  72.2 39.3 %all-gather.3 = f32[8192,8]{0,1:T(8,128)S(1)} all-gather(f32[256,8]{0,1:T(8,128)S(1)} %fusion.93), channel_id=2, replica_groups=mesh['section'=8,'expert'=8,'dp'=4] {'expert','dp'}, dimensions={0}, use_global_device_ids=true | all-gather | bytes 270336 | tf_op jit(solution)/shard_map/while/body/eval_jaxpr/all_gather | solution.py:13
  112.9 15.8 %all_to_all.58 = bf16[32,72,128]{2,1,0:T(8,128)(2,1)S(1)} all-to-all(bf16[32,72,128]{2,1,0:T(8,128)(2,1)S(1)} %bitcast.120), channel_id=1, replica_groups=mesh['section'=8,'expert'=8,'dp'=4] {'expert','dp'}, dimensions={0} | all-to-all | bytes 1179648 | tf_op jit(solution)/shard_map/while/body/eval_jaxpr/all_to_all | solution.py:102
  131.4 4.4 fusion.95
  135.9 16.2 %all_to_all.59 = bf16[72,32,128]{2,0,1:T(8,128)(2,1)S(1)} all-to-all(bf16[72,32,128]{2,0,1:T(8,128)(2,1)S(1)} %bitcast.122), channel_id=1, replica_groups=mesh['section'=8,'expert'=8,'dp'=4] {'expert','dp'}, dimensions={1} | all-to-all | bytes 1179648 | tf_op jit(solution)/shard_map/while/body/eval_jaxpr/all_to_all | solution.py:57
  155.2 5.6 collective-permute-done
  162.7 63.6 %psum.33 = f32[256]{0:T(256)S(1)} all-reduce(f32[256]{0:T(256)S(1)} %fusion.92), channel_id=1, replica_groups=mesh['section'=8,'expert'=8,'dp'=4] {'expert','dp'}, use_global_device_ids=true, to_apply=%region_5.5 | all-reduce | flops 256 | bytes 2048 | tf_op jit(solution)/shard_map/while/body/eval_jaxpr/psum | solution.py:75
  229.1 36.4 %all-gather.3 = f32[8192,8]{0,1:T(8,128)S(1)} all-gather(f32[256,8]{0,1:T(8,128)S(1)} %fusion.93), channel_id=2, replica_groups=mesh['section'=8,'expert'=8,'dp'=4] {'expert','dp'}, dimensions={0}, use_global_device_ids=true | all-gather | bytes 270336 | tf_op jit(solution)/shard_map/while/body/eval_jaxpr/all_gather | solution.py:13
  266.8 15.8 %all_to_all.58 = bf16[32,72,128]{2,1,0:T(8,128)(2,1)S(1)} all-to-all(bf16[32,72,128]{2,1,0:T(8,128)(2,1)S(1)} %bitcast.120), channel_id=1, replica_groups=mesh['section'=8,'expert'=8,'dp'=4] {'expert','dp'}, dimensions={0} | all-to-all | bytes 1179648 | tf_op jit(solution)/shard_map/while/body/eval_jaxpr/all_to_all | solution.py:102
  285.3 4.4 fusion.95
  289.8 16.2 %all_to_all.59 = bf16[72,32,128]{2,0,1:T(8,128)(2,1)S(1)} all-to-all(bf16[72,32,128]{2,0,1:T(8,128)(2,1)S(1)} %bitcast.122), channel_id=1, replica_groups=mesh['section'=8,'expert'=8,'dp'=4] {'expert','dp'}, dimensions={1} | all-to-all | bytes 1179648 | tf_op jit(solution)/shard_map/while/body/eval_jaxpr/all_to_all | solution.py:57
  307.5 4.3 collective-permute-done
  313.7 63.9 %psum.33 = f32[256]{0:T(256)S(1)} all-reduce(f32[256]{0:T(256)S(1)} %fusion.92), channel_id=1, replica_groups=mesh['section'=8,'expert'=8,'dp'=4] {'expert','dp'}, use_global_device_ids=true, to_apply=%region_5.5 | all-reduce | flops 256 | bytes 2048 | tf_op jit(solution)/shard_map/while/body/eval_jaxpr/psum | solution.py:75
  380.4 36.4 %all-gather.3 = f32[8192,8]{0,1:T(8,128)S(1)} all-gather(f32[256,8]{0,1:T(8,128)S(1)} %fusion.93), channel_id=2, replica_groups=mesh['section'=8,'expert'=8,'dp'=4] {'expert','dp'}, dimensions={0}, use_global_device_ids=true | all-gather | bytes 270336 | tf_op jit(solution)/shard_map/while/body/eval_jaxpr/all_gather | solution.py:13
  418.1 15.8 %all_to_all.58 = bf16[32,72,128]{2,1,0:T(8,128)(2,1)S(1)} all-to-all(bf16[32,72,128]{2,1,0:T(8,128)(2,1)S(1)} %bitcast.120), channel_id=1, replica_groups=mesh['section'=8,'expert'=8,'dp'=4] {'expert','dp'}, dimensions={0} | all-to-all | bytes 1179648 | tf_op jit(solution)/shard_map/while/body/eval_jaxpr/all_to_all | solution.py:102
  436.6 4.4 fusion.95
  441.1 16.2 %all_to_all.59 = bf16[72,32,128]{2,0,1:T(8,128)(2,1)S(1)} all-to-all(bf16[72,32,128]{2,0,1:T(8,128)(2,1)S(1)} %bitcast.122), channel_id=1, replica_groups=mesh['section'=8,'expert'=8,'dp'=4] {'expert','dp'}, dimensions={1} | all-to-all | bytes 1179648 | tf_op jit(solution)/shard_map/while/body/eval_jaxpr/all_to_all | solution.py:57
  458.8 4.3 collective-permute-done
  465.1 63.9 %psum.33 = f32[256]{0:T(256)S(1)} all-reduce(f32[256]{0:T(256)S(1)} %fusion.92), channel_id=1, replica_groups=mesh['section'=8,'expert'=8,'dp'=4] {'expert','dp'}, use_global_device_ids=true, to_apply=%region_5.5 | all-reduce | flops 256 | bytes 2048 | tf_op jit(solution)/shard_map/while/body/eval_jaxpr/psum | solution.py:75
  531.7 36.4 %all-gather.3 = f32[8192,8]{0,1:T(8,128)S(1)} all-gather(f32[256,8]{0,1:T(8,128)S(1)} %fusion.93), channel_id=2, replica_groups=mesh['section'=8,'expert'=8,'dp'=4] {'expert','dp'}, dimensions={0}, use_global_device_ids=true | all-gather | bytes 270336 | tf_op jit(solution)/shard_map/while/body/eval_jaxpr/all_gather | solution.py:13
  569.4 15.8 %all_to_all.58 = bf16[32,72,128]{2,1,0:T(8,128)(2,1)S(1)} all-to-all(bf16[32,72,128]{2,1,0:T(8,128)(2,1)S(1)} %bitcast.120), channel_id=1, replica_groups=mesh['section'=8,'expert'=8,'dp'=4] {'expert','dp'}, dimensions={0} | all-to-all | bytes 1179648 | tf_op jit(solution)/shard_map/while/body/eval_jaxpr/all_to_all | solution.py:102
  587.9 4.4 fusion.95
  592.4 16.2 %all_to_all.59 = bf16[72,32,128]{2,0,1:T(8,128)(2,1)S(1)} all-to-all(bf16[72,32,128]{2,0,1:T(8,128)(2,1)S(1)} %bitcast.122), channel_id=1, replica_groups=mesh['section'=8,'expert'=8,'dp'=4] {'expert','dp'}, dimensions={1} | all-to-all | bytes 1179648 | tf_op jit(solution)/shard_map/while/body/eval_jaxpr/all_to_all | solution.py:57
  616.4 63.9 %psum.33 = f32[256]{0:T(256)S(1)} all-reduce(f32[256]{0:T(256)S(1)} %fusion.92), channel_id=1, replica_groups=mesh['section'=8,'expert'=8,'dp'=4] {'expert','dp'}, use_global_device_ids=true, to_apply=%region_5.5 | all-reduce | flops 256 | bytes 2048 | tf_op jit(solution)/shard_map/while/body/eval_jaxpr/psum | solution.py:75
  683.0 36.4 %all-gather.3 = f32[8192,8]{0,1:T(8,128)S(1)} all-gather(f32[256,8]{0,1:T(8,128)S(1)} %fusion.93), channel_id=2, replica_groups=mesh['section'=8,'expert'=8,'dp'=4] {'expert','dp'}, dimensions={0}, use_global_device_ids=true | all-gather | bytes 270336 | tf_op jit(solution)/shard_map/while/body/eval_jaxpr/all_gather | solution.py:13
  720.7 15.8 %all_to_all.58 = bf16[32,72,128]{2,1,0:T(8,128)(2,1)S(1)} all-to-all(bf16[32,72,128]{2,1,0:T(8,128)(2,1)S(1)} %bitcast.120), channel_id=1, replica_groups=mesh['section'=8,'expert'=8,'dp'=4] {'expert','dp'}, dimensions={0} | all-to-all | bytes 1179648 | tf_op jit(solution)/shard_map/while/body/eval_jaxpr/all_to_all | solution.py:102
  739.2 4.4 fusion.95
  743.7 16.2 %all_to_all.59 = bf16[72,32,128]{2,0,1:T(8,128)(2,1)S(1)} all-to-all(bf16[72,32,128]{2,0,1:T(8,128)(2,1)S(1)} %bitcast.122), channel_id=1, replica_groups=mesh['section'=8,'expert'=8,'dp'=4] {'expert','dp'}, dimensions={1} | all-to-all | bytes 1179648 | tf_op jit(solution)/shard_map/while/body/eval_jaxpr/all_to_all | solution.py:57
  761.4 4.3 collective-permute-done
  767.7 63.9 %psum.33 = f32[256]{0:T(256)S(1)} all-reduce(f32[256]{0:T(256)S(1)} %fusion.92), channel_id=1, replica_groups=mesh['section'=8,'expert'=8,'dp'=4] {'expert','dp'}, use_global_device_ids=true, to_apply=%region_5.5 | all-reduce | flops 256 | bytes 2048 | tf_op jit(solution)/shard_map/while/body/eval_jaxpr/psum | solution.py:75
  834.3 36.4 %all-gather.3 = f32[8192,8]{0,1:T(8,128)S(1)} all-gather(f32[256,8]{0,1:T(8,128)S(1)} %fusion.93), channel_id=2, replica_groups=mesh['section'=8,'expert'=8,'dp'=4] {'expert','dp'}, dimensions={0}, use_global_device_ids=true | all-gather | bytes 270336 | tf_op jit(solution)/shard_map/while/body/eval_jaxpr/all_gather | solution.py:13
  872.0 15.8 %all_to_all.58 = bf16[32,72,128]{2,1,0:T(8,128)(2,1)S(1)} all-to-all(bf16[32,72,128]{2,1,0:T(8,128)(2,1)S(1)} %bitcast.120), channel_id=1, replica_groups=mesh['section'=8,'expert'=8,'dp'=4] {'expert','dp'}, dimensions={0} | all-to-all | bytes 1179648 | tf_op jit(solution)/shard_map/while/body/eval_jaxpr/all_to_all | solution.py:102
  890.5 4.4 fusion.95
  895.0 16.2 %all_to_all.59 = bf16[72,32,128]{2,0,1:T(8,128)(2,1)S(1)} all-to-all(bf16[72,32,128]{2,0,1:T(8,128)(2,1)S(1)} %bitcast.122), channel_id=1, replica_groups=mesh['section'=8,'expert'=8,'dp'=4] {'expert','dp'}, dimensions={1} | all-to-all | bytes 1179648 | tf_op jit(solution)/shard_map/while/body/eval_jaxpr/all_to_all | solution.py:57
  912.7 4.3 collective-permute-done
  919.0 63.9 %psum.33 = f32[256]{0:T(256)S(1)} all-reduce(f32[256]{0:T(256)S(1)} %fusion.92), channel_id=1, replica_groups=mesh['section'=8,'expert'=8,'dp'=4] {'expert','dp'}, use_global_device_ids=true, to_apply=%region_5.5 | all-reduce | flops 256 | bytes 2048 | tf_op jit(solution)/shard_map/while/body/eval_jaxpr/psum | solution.py:75
  985.6 36.4 %all-gather.3 = f32[8192,8]{0,1:T(8,128)S(1)} all-gather(f32[256,8]{0,1:T(8,128)S(1)} %fusion.93), channel_id=2, replica_groups=mesh['section'=8,'expert'=8,'dp'=4] {'expert','dp'}, dimensions={0}, use_global_device_ids=true | all-gather | bytes 270336 | tf_op jit(solution)/shard_map/while/body/eval_jaxpr/all_gather | solution.py:13
  1023.3 15.8 %all_to_all.58 = bf16[32,72,128]{2,1,0:T(8,128)(2,1)S(1)} all-to-all(bf16[32,72,128]{2,1,0:T(8,128)(2,1)S(1)} %bitcast.120), channel_id=1, replica_groups=mesh['section'=8,'expert'=8,'dp'=4] {'expert','dp'}, dimensions={0} | all-to-all | bytes 1179648 | tf_op jit(solution)/shard_map/while/body/eval_jaxpr/all_to_all | solution.py:102
  1041.8 4.4 fusion.95
  1046.3 16.2 %all_to_all.59 = bf16[72,32,128]{2,0,1:T(8,128)(2,1)S(1)} all-to-all(bf16[72,32,128]{2,0,1:T(8,128)(2,1)S(1)} %bitcast.122), channel_id=1, replica_groups=mesh['section'=8,'expert'=8,'dp'=4] {'expert','dp'}, dimensions={1} | all-to-all | bytes 1179648 | tf_op jit(solution)/shard_map/while/body/eval_jaxpr/all_to_all | solution.py:57
  1064.0 4.3 collective-permute-done
  1070.3 63.9 %psum.33 = f32[256]{0:T(256)S(1)} all-reduce(f32[256]{0:T(256)S(1)} %fusion.92), channel_id=1, replica_groups=mesh['section'=8,'expert'=8,'dp'=4] {'expert','dp'}, use_global_device_ids=true, to_apply=%region_5.5 | all-reduce | flops 256 | bytes 2048 | tf_op jit(solution)/shard_map/while/body/eval_jaxpr/psum | solution.py:75
  1136.9 36.4 %all-gather.3 = f32[8192,8]{0,1:T(8,128)S(1)} all-gather(f32[256,8]{0,1:T(8,128)S(1)} %fusion.93), channel_id=2, replica_groups=mesh['section'=8,'expert'=8,'dp'=4] {'expert','dp'}, dimensions={0}, use_global_device_ids=true | all-gather | bytes 270336 | tf_op jit(solution)/shard_map/while/body/eval_jaxpr/all_gather | solution.py:13
  1174.6 15.8 %all_to_all.58 = bf16[32,72,128]{2,1,0:T(8,128)(2,1)S(1)} all-to-all(bf16[32,72,128]{2,1,0:T(8,128)(2,1)S(1)} %bitcast.120), channel_id=1, replica_groups=mesh['section'=8,'expert'=8,'dp'=4] {'expert','dp'}, dimensions={0} | all-to-all | bytes 1179648 | tf_op jit(solution)/shard_map/while/body/eval_jaxpr/all_to_all | solution.py:102
  1193.1 4.4 fusion.95
  1197.6 16.2 %all_to_all.59 = bf16[72,32,128]{2,0,1:T(8,128)(2,1)S(1)} all-to-all(bf16[72,32,128]{2,0,1:T(8,128)(2,1)S(1)} %bitcast.122), channel_id=1, replica_groups=mesh['section'=8,'expert'=8,'dp'=4] {'expert','dp'}, dimensions={1} | all-to-all | bytes 1179648 | tf_op jit(solution)/shard_map/while/body/eval_jaxpr/all_to_all | solution.py:57
  1219.9 72.8 %all-reduce = (f32[8]{0:T(128)S(1)}, f32[8]{0:T(128)S(1)}) all-reduce(f32[8]{0:T(128)S(1)} %broadcast_multiply_fusion.1, f32[8]{0:T(128)S(1)} %convolution_bitcast_fusion.1), channel_id=1, replica_groups=mesh['section'=8,'expert'=8,'dp'=4] {'section','expert','dp'}, use_global_device_ids=true, to_apply=%region_16.17 | all-reduce | flops 16 | bytes 128 | tf_op jit(solution)/shard_map/psum | solution.py:126
  (265 shorter events, 95.2 us)
Async XLA Ops:
  2.3 1217.4 %copy-start = (bf16[1,256,128]{2,1,0:T(8,128)(2,1)S(1)}, bf16[1,256,128]{2,1,0:T(8,128)(2,1)}, u32[]{:S(2)}) copy-start(bf16[1,256,128]{2,1,0:T(8,128)(2,1)} %param.12) | copy-start | bytes 196612
  2.3 1217.5 %copy-start.2 = (s32[1,256]{1,0:T(1,128)S(1)}, s32[1,256]{1,0:T(1,128)}, u32[]{:S(2)}) copy-start(s32[1,256]{1,0:T(1,128)} %param.13) | copy-start | bytes 3076
  153.5 7.3 collective-permute-start
  307.4 4.4 collective-permute-start
  458.7 4.4 collective-permute-start
  610.0 4.4 collective-permute-start
  761.3 4.4 collective-permute-start
  912.6 4.4 collective-permute-start
  1063.9 4.4 collective-permute-start
  1215.2 4.4 collective-permute-start
  1293.3 1.5 copy-start.1
